TPU v7x, 32 devices: a whole 2x2x4 slice. The times are simulated.
32 devices in a mesh: dp: 8 (over y, x, core), fsdp: 4 (over z).
Axes of the slice: x: 2, y: 2, z: 4, core: 2. Of those that a mesh axis runs over, the one named last changes fastest.
Arguments:
- tokens: bfloat16 [32, 256, 1152], P(('dp', 'fsdp')), may hold values from -6 to 6
- condition: bfloat16 [32, 1152], P(('dp', 'fsdp')), may hold values from -6 to 6
- grid_sizes: int32 [32, 2], P(('dp', 'fsdp')), may hold values from 12 to 20, as said below
- w_ada: bfloat16 [1152, 6912], P('fsdp'), may hold values from -0.1875 to 0.1875
- w_qkv: bfloat16 [1152, 3456], P('fsdp'), may hold values from -0.1875 to 0.1875
- w_out: bfloat16 [1152, 1152], P('fsdp'), may hold values from -1 to 1
- w_up: bfloat16 [1152, 4608], P('fsdp'), may hold values from -0.1875 to 0.1875
- w_down: bfloat16 [4608, 1152], P('fsdp'), may hold values from -0.09375 to 0.09375
- b_ada: bfloat16 [6912], P('fsdp'), may hold values from -3 to 3
- b_qv: bfloat16 [2304], P('fsdp'), may hold values from -3 to 3
- b_out: bfloat16 [1152], P('fsdp'), may hold values from -3 to 3
- b_up: bfloat16 [4608], P('fsdp'), may hold values from -3 to 3
- b_down: bfloat16 [1152], P('fsdp'), may hold values from -3 to 3
- cotangent: bfloat16 [32, 256, 1152], P(('dp', 'fsdp')), may hold values from -6 to 6
Outputs:
- output: bfloat16 [32, 256, 1152], P(('dp', 'fsdp'))
- grad_tokens: bfloat16 [32, 256, 1152], P(('dp', 'fsdp'))
- grad_condition: float32 [32, 1152], P(('dp', 'fsdp'))
- grad_w_ada: float32 [1152, 6912], P('fsdp', 'dp')
- grad_w_qkv: float32 [1152, 3456], P('fsdp', 'dp')
- grad_w_out: float32 [1152, 1152], P('fsdp', 'dp')
- grad_w_up: float32 [1152, 4608], P('fsdp', 'dp')
- grad_w_down: float32 [4608, 1152], P('fsdp', 'dp')
- grad_b_ada: float32 [6912], P('fsdp')
- grad_b_qv: float32 [2304], P('fsdp')
- grad_b_out: float32 [1152], P('fsdp')
- grad_b_up: float32 [4608], P('fsdp')
- grad_b_down: float32 [1152], P('fsdp')
Inputs may be any that keep to these rules, and one draw needn't show every extreme that they name: `grid_sizes`: each image grid has 12 to 20 rows and columns and at most 256 tokens; image 0 has 12 rows and 20 columns, and image 1 has 20 rows and 12 columns.
All inputs are finite; a program needn't handle non-finite values.
Results may differ from a plain program's by a relative error of at most 0.015.
The roundings to bfloat16 on the way count: a program that leaves them out, or rounds other values in their place, can miss the bound.
Values may be sent and summed in bfloat16 or wider, within the bound.
No kernel may reach another device: no remote copies, remote signals or barrier semaphores. Data moves between devices by JAX's collectives and lax.ppermute only.
A program may use at most 256 MiB of HBM per device.

v0:
```python
import math
import jax
import jax.numpy as jnp
from jax import lax
from jax.sharding import PartitionSpec as P

HEAD_DIM = 72
epsilon = 1e-06
masked_value = -1e30
gelu_root = math.sqrt(2.0 / math.pi)


def layer_norm(values_in):
    centred = values_in - jnp.mean(values_in, axis=-1, keepdims=True)
    spread = jnp.mean(centred * centred, axis=-1, keepdims=True)
    return centred * lax.rsqrt(spread + epsilon)


def gelu_tanh(pre_act):
    return (
        0.5
        * pre_act
        * (1.0 + jnp.tanh(gelu_root * (pre_act + 0.044715 * pre_act * pre_act * pre_act)))
    )


def apply_rows(left, right):
    return jnp.einsum("isd,de->ise", left, right, preferred_element_type=jnp.float32)


def forward_pass(weights_full, tokens_wide, cond_act, live_keys, kept_lse):
    w_ada, w_qkv, w_out, w_up, w_down, b_ada, b_qv, b_out, b_up, b_down = weights_full
    width = w_out.shape[0]
    images = tokens_wide.shape[0]
    slots = tokens_wide.shape[1]
    heads = width // HEAD_DIM
    modulation = jnp.dot(cond_act, w_ada, preferred_element_type=jnp.float32) + b_ada.astype(
        jnp.float32
    )
    portions = jnp.split(modulation, 6, axis=1)
    modulated = tuple((portion[:, None, :] for portion in portions))
    shift_one, scale_one, gate_one, shift_two, scale_two, gate_two = modulated
    norm_one = layer_norm(tokens_wide)
    normed = (norm_one * (1.0 + scale_one) + shift_one).astype(jnp.bfloat16)
    projected = apply_rows(normed, w_qkv)
    bias_qv = b_qv.astype(jnp.float32)
    queries = (
        (projected[..., :width] + bias_qv[:width])
        .astype(jnp.bfloat16)
        .reshape(images, slots, heads, HEAD_DIM)
    )
    key_part = (
        projected[..., width : 2 * width]
        .astype(jnp.bfloat16)
        .reshape(images, slots, heads, HEAD_DIM)
    )
    values = (
        (projected[..., 2 * width :] + bias_qv[width:])
        .astype(jnp.bfloat16)
        .reshape(images, slots, heads, HEAD_DIM)
    )
    raw = jnp.einsum(
        "iqhe,ikhe->ihqk", queries, key_part, preferred_element_type=jnp.float32
    ) * HEAD_DIM ** (-0.5)
    scores = jnp.where(live_keys[:, None, None, :], raw, masked_value)
    if kept_lse is None:
        highest = jnp.max(scores, axis=-1, keepdims=True)
        lse = highest + jnp.log(jnp.sum(jnp.exp(scores - highest), axis=-1, keepdims=True))
    else:
        lse = kept_lse
    probs = jnp.exp(scores - lse)
    probs_low = probs.astype(jnp.bfloat16)
    attended = jnp.einsum("ihqk,ikhe->iqhe", probs_low, values, preferred_element_type=jnp.float32)
    attended = attended.reshape(images, slots, width).astype(jnp.bfloat16)
    attn_out = apply_rows(attended, w_out) + b_out.astype(jnp.float32)
    middle = tokens_wide + gate_one * attn_out
    norm_two = layer_norm(middle)
    normed_two = (norm_two * (1.0 + scale_two) + shift_two).astype(jnp.bfloat16)
    pre_act = apply_rows(normed_two, w_up) + b_up.astype(jnp.float32)
    activated = gelu_tanh(pre_act).astype(jnp.bfloat16)
    mlp_out = apply_rows(activated, w_down) + b_down.astype(jnp.float32)
    return (
        modulated,
        norm_one,
        normed,
        queries,
        key_part,
        values,
        lse,
        probs,
        probs_low,
        attended,
        attn_out,
        middle,
        norm_two,
        normed_two,
        pre_act,
        activated,
        mlp_out,
    )


def body(
    tokens,
    condition,
    grid_sizes,
    w_ada,
    w_qkv,
    w_out,
    w_up,
    w_down,
    b_ada,
    b_qv,
    b_out,
    b_up,
    b_down,
    cotangent,
):
    weights_full = (
        lax.all_gather(w_ada, "fsdp", axis=0, tiled=True),
        lax.all_gather(w_qkv, "fsdp", axis=0, tiled=True),
        lax.all_gather(w_out, "fsdp", axis=0, tiled=True),
        lax.all_gather(w_up, "fsdp", axis=0, tiled=True),
        lax.all_gather(w_down, "fsdp", axis=0, tiled=True),
        lax.all_gather(b_ada, "fsdp", axis=0, tiled=True),
        lax.all_gather(b_qv, "fsdp", axis=0, tiled=True),
        lax.all_gather(b_out, "fsdp", axis=0, tiled=True),
        lax.all_gather(b_up, "fsdp", axis=0, tiled=True),
        lax.all_gather(b_down, "fsdp", axis=0, tiled=True),
    )
    images = tokens.shape[0]
    slots = tokens.shape[1]
    width = tokens.shape[2]
    heads = width // HEAD_DIM
    live_counts = grid_sizes[:, 0] * grid_sizes[:, 1]
    live_keys = lax.broadcasted_iota(jnp.int32, (images, slots), 1) < live_counts[:, None]
    live_rows = live_keys.astype(jnp.float32)[:, :, None]
    tokens_wide = tokens.astype(jnp.float32)
    cond_wide = condition.astype(jnp.float32)
    cond_act = (cond_wide * jax.nn.sigmoid(cond_wide)).astype(jnp.bfloat16)
    saved = forward_pass(weights_full, tokens_wide, cond_act, live_keys, None)
    middle_first = saved[11]
    gate_first = saved[0][5]
    mlp_first = saved[16]
    output = (live_rows * (middle_first + gate_first * mlp_first)).astype(jnp.bfloat16)
    weights_back = (
        lax.all_gather(w_ada, "fsdp", axis=0, tiled=True),
        lax.all_gather(w_qkv, "fsdp", axis=0, tiled=True),
        lax.all_gather(w_out, "fsdp", axis=0, tiled=True),
        lax.all_gather(w_up, "fsdp", axis=0, tiled=True),
        lax.all_gather(w_down, "fsdp", axis=0, tiled=True),
        lax.all_gather(b_ada, "fsdp", axis=0, tiled=True),
        lax.all_gather(b_qv, "fsdp", axis=0, tiled=True),
        lax.all_gather(b_out, "fsdp", axis=0, tiled=True),
        lax.all_gather(b_up, "fsdp", axis=0, tiled=True),
        lax.all_gather(b_down, "fsdp", axis=0, tiled=True),
    )
    saved = forward_pass(weights_back, tokens_wide, cond_act, live_keys, saved[6])
    (
        modulated,
        norm_one,
        normed,
        queries,
        key_part,
        values,
        lse,
        probs,
        probs_low,
        attended,
        attn_out,
        middle,
        norm_two,
        normed_two,
        pre_act,
        activated,
        mlp_out,
    ) = saved
    shift_one, scale_one, gate_one, shift_two, scale_two, gate_two = modulated
    ada_full, qkv_full, out_full, up_full, down_full = (
        weights_back[0],
        weights_back[1],
        weights_back[2],
        weights_back[3],
        weights_back[4],
    )
    upstream = live_rows * cotangent.astype(jnp.float32)
    d_gate_two = jnp.sum(upstream * mlp_out, axis=1)
    d_mlp = (gate_two * upstream).astype(jnp.bfloat16)
    grad_w_down = jnp.einsum("isf,isd->fd", activated, d_mlp, preferred_element_type=jnp.float32)
    grad_b_down = jnp.sum(d_mlp.astype(jnp.float32), axis=(0, 1))
    d_act = jnp.einsum("isd,fd->isf", d_mlp, down_full, preferred_element_type=jnp.float32)
    unused_gelu, gelu_pull = jax.vjp(gelu_tanh, pre_act)
    d_pre = gelu_pull(d_act)[0].astype(jnp.bfloat16)
    grad_w_up = jnp.einsum("isd,isf->df", normed_two, d_pre, preferred_element_type=jnp.float32)
    grad_b_up = jnp.sum(d_pre.astype(jnp.float32), axis=(0, 1))
    d_normed_two = jnp.einsum("isf,df->isd", d_pre, up_full, preferred_element_type=jnp.float32)
    d_shift_two = jnp.sum(d_normed_two, axis=1)
    d_scale_two = jnp.sum(d_normed_two * norm_two, axis=1)
    unused_norm, second_pull = jax.vjp(layer_norm, middle)
    d_middle = upstream + second_pull(d_normed_two * (1.0 + scale_two))[0]
    d_gate_one = jnp.sum(d_middle * attn_out, axis=1)
    d_attn = (gate_one * d_middle).astype(jnp.bfloat16)
    grad_w_out = jnp.einsum("isd,ise->de", attended, d_attn, preferred_element_type=jnp.float32)
    grad_b_out = jnp.sum(d_attn.astype(jnp.float32), axis=(0, 1))
    d_attended = jnp.einsum("ise,de->isd", d_attn, out_full, preferred_element_type=jnp.float32)
    d_attended = d_attended.astype(jnp.bfloat16).reshape(images, slots, heads, HEAD_DIM)
    d_probs = jnp.einsum("iqhe,ikhe->ihqk", d_attended, values, preferred_element_type=jnp.float32)
    d_values = jnp.einsum(
        "ihqk,iqhe->ikhe", probs_low, d_attended, preferred_element_type=jnp.float32
    ).astype(jnp.bfloat16)
    row_inner = jnp.sum(probs * d_probs, axis=-1, keepdims=True)
    d_scores = (probs * (d_probs - row_inner)).astype(jnp.bfloat16)
    d_queries = (
        jnp.einsum("ihqk,ikhe->iqhe", d_scores, key_part, preferred_element_type=jnp.float32)
        * HEAD_DIM ** (-0.5)
    ).astype(jnp.bfloat16)
    d_keys = (
        jnp.einsum("ihqk,iqhe->ikhe", d_scores, queries, preferred_element_type=jnp.float32)
        * HEAD_DIM ** (-0.5)
    ).astype(jnp.bfloat16)
    d_projected = jnp.concatenate(
        [
            d_queries.reshape(images, slots, width),
            d_keys.reshape(images, slots, width),
            d_values.reshape(images, slots, width),
        ],
        axis=2,
    )
    grad_w_qkv = jnp.einsum("isd,ise->de", normed, d_projected, preferred_element_type=jnp.float32)
    grad_b_qv = jnp.concatenate(
        [
            jnp.sum(d_queries.astype(jnp.float32), axis=(0, 1)).reshape(width),
            jnp.sum(d_values.astype(jnp.float32), axis=(0, 1)).reshape(width),
        ]
    )
    d_normed = jnp.einsum("ise,de->isd", d_projected, qkv_full, preferred_element_type=jnp.float32)
    d_shift_one = jnp.sum(d_normed, axis=1)
    d_scale_one = jnp.sum(d_normed * norm_one, axis=1)
    unused_first, first_pull = jax.vjp(layer_norm, tokens_wide)
    grad_tokens = (d_middle + first_pull(d_normed * (1.0 + scale_one))[0]).astype(jnp.bfloat16)
    d_modulation = jnp.concatenate(
        [d_shift_one, d_scale_one, d_gate_one, d_shift_two, d_scale_two, d_gate_two], axis=1
    ).astype(jnp.bfloat16)
    grad_w_ada = jnp.einsum("id,ie->de", cond_act, d_modulation, preferred_element_type=jnp.float32)
    grad_b_ada = jnp.sum(d_modulation.astype(jnp.float32), axis=0)
    d_cond_act = jnp.einsum("ie,de->id", d_modulation, ada_full, preferred_element_type=jnp.float32)
    unused_silu, silu_pull = jax.vjp(lambda inner: inner * jax.nn.sigmoid(inner), cond_wide)
    grad_condition = silu_pull(d_cond_act)[0]
    narrow = (
        lax.psum_scatter(
            grad_w_ada.astype(jnp.bfloat16), "fsdp", scatter_dimension=0, tiled=True
        ).astype(jnp.float32),
        lax.psum_scatter(
            grad_w_qkv.astype(jnp.bfloat16), "fsdp", scatter_dimension=0, tiled=True
        ).astype(jnp.float32),
        lax.psum_scatter(
            grad_w_out.astype(jnp.bfloat16), "fsdp", scatter_dimension=0, tiled=True
        ).astype(jnp.float32),
        lax.psum_scatter(
            grad_w_up.astype(jnp.bfloat16), "fsdp", scatter_dimension=0, tiled=True
        ).astype(jnp.float32),
        lax.psum_scatter(
            grad_w_down.astype(jnp.bfloat16), "fsdp", scatter_dimension=0, tiled=True
        ).astype(jnp.float32),
        lax.psum_scatter(
            grad_b_ada.astype(jnp.bfloat16), "fsdp", scatter_dimension=0, tiled=True
        ).astype(jnp.float32),
        lax.psum_scatter(
            grad_b_qv.astype(jnp.bfloat16), "fsdp", scatter_dimension=0, tiled=True
        ).astype(jnp.float32),
        lax.psum_scatter(
            grad_b_out.astype(jnp.bfloat16), "fsdp", scatter_dimension=0, tiled=True
        ).astype(jnp.float32),
        lax.psum_scatter(
            grad_b_up.astype(jnp.bfloat16), "fsdp", scatter_dimension=0, tiled=True
        ).astype(jnp.float32),
        lax.psum_scatter(
            grad_b_down.astype(jnp.bfloat16), "fsdp", scatter_dimension=0, tiled=True
        ).astype(jnp.float32),
    )
    summed_weights = (
        lax.psum_scatter(narrow[0], "dp", scatter_dimension=1, tiled=True),
        lax.psum_scatter(narrow[1], "dp", scatter_dimension=1, tiled=True),
        lax.psum_scatter(narrow[2], "dp", scatter_dimension=1, tiled=True),
        lax.psum_scatter(narrow[3], "dp", scatter_dimension=1, tiled=True),
        lax.psum_scatter(narrow[4], "dp", scatter_dimension=1, tiled=True),
    )
    summed_biases = lax.psum((narrow[5], narrow[6], narrow[7], narrow[8], narrow[9]), "dp")
    return (
        output,
        grad_tokens,
        grad_condition,
        summed_weights[0],
        summed_weights[1],
        summed_weights[2],
        summed_weights[3],
        summed_weights[4],
        summed_biases[0],
        summed_biases[1],
        summed_biases[2],
        summed_biases[3],
        summed_biases[4],
    )


def solution(mesh):
    return jax.shard_map(
        body,
        mesh=mesh,
        in_specs=(
            P(("dp", "fsdp"), None, None),
            P(("dp", "fsdp"), None),
            P(("dp", "fsdp"), None),
            P("fsdp", None),
            P("fsdp", None),
            P("fsdp", None),
            P("fsdp", None),
            P("fsdp", None),
            P("fsdp"),
            P("fsdp"),
            P("fsdp"),
            P("fsdp"),
            P("fsdp"),
            P(("dp", "fsdp"), None, None),
        ),
        out_specs=(
            P(("dp", "fsdp"), None, None),
            P(("dp", "fsdp"), None, None),
            P(("dp", "fsdp"), None),
            P("fsdp", "dp"),
            P("fsdp", "dp"),
            P("fsdp", "dp"),
            P("fsdp", "dp"),
            P("fsdp", "dp"),
            P("fsdp"),
            P("fsdp"),
            P("fsdp"),
            P("fsdp"),
            P("fsdp"),
        ),
        check_vma=False,
    )
```

profile of v0, /device:TPU:0, one launch (start us, length us, event | category | flops | bytes accessed | tf_op | source)
XLA Modules:
  0.0 2053.4 jit_solution(9514321274415671537)
XLA Ops:
  14.4 21.8 %all-reduce.11 = (bf16[2304]{0:T(1024)(128)(2,1)S(1)}, bf16[6912]{0:T(1024)(128)(2,1)S(1)}, bf16[1152]{0:T(1024)(128)(2,1)S(1)}, bf16[1152]{0:T(1024)(128)(2,1)}) all-reduce(bf16[2304]{0:T(1024)(128)(2,1)S(1)} %dynamic-update-slice.1, bf16[6912]{0:T(1024)(128)(2,1)S(1)} %dynamic-update-slice, ...), channel_id=1, replica_groups=mesh['dp'=8,'fsdp'=4] {'fsdp'}, use_global_device_ids=true, to_apply=%add.1 | all-reduce | flops 11520 | bytes 46080
  36.8 17.0 all-gather
  58.1 227.6 %all-gather.7.cloned.1.call-done = bf16[1152,6912]{1,0:T(8,128)(2,1)} async-done(((bf16[288,6912]{1,0:T(8,128)(2,1)}), bf16[1152,6912]{1,0:T(8,128)(2,1)}) %all-gather.7.cloned.1.call-update) | async-done | bytes 15925264 | tf_op jit(solution)/shard_map/all_gather | solution.py:120
  285.7 7.7 convolution_reduce_fusion
  294.2 134.1 %all-gather.9.cloned.1.call-done = bf16[1152,3456]{1,0:T(8,128)(2,1)} async-done(((bf16[288,3456]{1,0:T(8,128)(2,1)}), bf16[1152,3456]{1,0:T(8,128)(2,1)}) %all-gather.9.cloned.1.call-update) | async-done | bytes 7962640 | tf_op jit(solution)/shard_map/all_gather | solution.py:121
  428.3 6.0 convolution_bitcast_fusion
  434.3 0.9 slice.46
  435.8 1.3 copy.53
  437.1 1.1 fusion.6
  438.3 1.0 exponential_reduce_fusion
  439.3 0.9 copy-done
  440.2 1.7 convolution_convert_fusion.6
  441.9 41.5 %all-gather.11.cloned.1.call-done = bf16[1152,1152]{1,0:T(8,128)(2,1)} async-done(((bf16[288,1152]{1,0:T(8,128)(2,1)}), bf16[1152,1152]{1,0:T(8,128)(2,1)}) %all-gather.11.cloned.1.call-update) | async-done | bytes 2654224 | tf_op jit(solution)/shard_map/all_gather | solution.py:122
  483.4 3.9 fusion.60
  489.3 180.4 %all-gather.13.cloned.1.call-done = bf16[1152,4608]{1,0:T(8,128)(2,1)} async-done(((bf16[288,4608]{1,0:T(8,128)(2,1)}), bf16[1152,4608]{1,0:T(8,128)(2,1)}) %all-gather.13.cloned.1.call-update) | async-done | bytes 10616848 | tf_op jit(solution)/shard_map/all_gather | solution.py:123
  669.7 9.3 convolution_add_fusion
  679.0 176.4 %all-gather.15.cloned.1.call-done = bf16[4608,1152]{1,0:T(8,128)(2,1)} async-done(((bf16[1152,1152]{1,0:T(8,128)(2,1)}), bf16[4608,1152]{1,0:T(8,128)(2,1)}) %all-gather.15.cloned.1.call-update) | async-done | bytes 10616848 | tf_op jit(solution)/shard_map/all_gather | solution.py:124
  855.4 10.1 fusion.64
  865.5 8.8 fusion.24
  874.8 1.0 copy-done.15
  875.8 1.0 fusion.58
  877.7 1.9 convolution_convert_fusion.4
  879.5 2.1 copy.55
  881.7 4.3 bitcast_reduce_fusion
  886.0 1.5 multiply_reduce_fusion
  887.5 1.4 multiply_convert_fusion.2
  889.7 1.2 bitcast_reduce_fusion.1
  891.7 5.8 convolution_convert_fusion.2
  898.2 8.7 convolution_convert_fusion.1
  907.0 1.4 convert_element_type.228
  908.4 1.3 convert.45
  910.3 7.0 fusion.20
  918.0 0.9 dynamic-update-slice.4
  919.6 1.9 fusion.18
  921.5 0.9 dynamic-update-slice.5
  923.1 11.8 fusion.23
  934.8 0.9 dynamic-update-slice.6
  935.7 0.9 dynamic-update-slice.7
  936.6 0.9 dynamic-update-slice.8
  937.4 0.9 dynamic-update-slice.9
  938.3 6.6 multiply_convert_fusion
  946.0 2.4 convolution_convert_fusion.3
  948.5 1.0 copy-done.16
  949.4 10.6 convolution_convert_fusion
  960.1 73.8 %reduce-scatter.23.cloned.1.call-done = bf16[288,3456]{1,0:T(8,128)(2,1)} async-done(((bf16[1152,3456]{1,0:T(8,128)(2,1)}), bf16[288,3456]{1,0:T(8,128)(2,1)}) %reduce-scatter.23.cloned.1.call-update) | async-done | bytes 1990672 | tf_op jit(solution)/shard_map/reduce_scatter | solution.py:253
  1034.0 4.5 copy.67
  1038.5 178.7 %reduce-scatter.27.cloned.1.call-done = bf16[288,4608]{1,0:T(8,128)(2,1)} async-done(((bf16[1152,4608]{1,0:T(8,128)(2,1)}), bf16[288,4608]{1,0:T(8,128)(2,1)}) %reduce-scatter.27.cloned.1.call-update) | async-done | bytes 2654224 | tf_op jit(solution)/shard_map/reduce_scatter | solution.py:259
  1217.2 5.5 copy.71
  1222.8 265.3 %reduce-scatter.21.cloned.1.call-done = bf16[288,6912]{1,0:T(8,128)(2,1)} async-done(((bf16[1152,6912]{1,0:T(8,128)(2,1)}), bf16[288,6912]{1,0:T(8,128)(2,1)}) %reduce-scatter.21.cloned.1.call-update) | async-done | bytes 3981328 | tf_op jit(solution)/shard_map/reduce_scatter | solution.py:250
  1488.1 7.7 copy.65
  1495.8 47.9 %reduce-scatter.25.cloned.1.call-done = bf16[288,1152]{1,0:T(8,128)(2,1)} async-done(((bf16[1152,1152]{1,0:T(8,128)(2,1)}), bf16[288,1152]{1,0:T(8,128)(2,1)}) %reduce-scatter.25.cloned.1.call-update) | async-done | bytes 663568 | tf_op jit(solution)/shard_map/reduce_scatter | solution.py:256
  1543.7 2.6 copy.69
  1546.4 179.5 %reduce-scatter.29.cloned.1.call-done = bf16[1152,1152]{1,0:T(8,128)(2,1)} async-done(((bf16[4608,1152]{1,0:T(8,128)(2,1)}), bf16[1152,1152]{1,0:T(8,128)(2,1)}) %reduce-scatter.29.cloned.1.call-update) | async-done | bytes 2654224 | tf_op jit(solution)/shard_map/reduce_scatter | solution.py:262
  1725.9 5.4 copy.73
  1734.2 19.1 all-reduce.10
  1753.7 23.5 %all-reduce.9 = (f32[1728]{0:T(1024)}, f32[576]{0:T(1024)}, f32[288]{0:T(512)}, f32[1152]{0:T(1024)}, f32[288]{0:T(512)}) all-reduce(f32[1728]{0:T(1024)S(1)} %dynamic-slice_convert_fusion.1, f32[576]{0:T(1024)S(1)} %dynamic-slice_convert_fusion.2, f32[288]{0:T(512)S(1)} %get-tuple-element.112, ...), channel_id=1, replica_groups=mesh['dp'=8,'fsdp'=4] {'dp'}, use_global_device_ids=true, to_apply=%region_28.29 | all-reduce | flops 4032 | bytes 32256 | tf_op jit(solution)/shard_map/psum | solution.py:288
  1777.1 10.4 fusion.40
  1787.7 2.1 copy.68
  1789.8 67.2 %reduce-scatter.37.cloned.1.call-done = f32[576,288]{1,0:T(8,128)} async-done(((f32[4608,288]{1,0:T(8,128)}), f32[576,288]{1,0:T(8,128)}) %reduce-scatter.37.cloned.1.call-update) | async-done | bytes 663568
  1857.0 2.3 copy.72
  1859.3 83.4 %reduce-scatter.31.cloned.1.call-done = f32[864,288]{1,0:T(8,128)} async-done(((f32[6912,288]{1,0:T(8,128)}), f32[864,288]{1,0:T(8,128)}) %reduce-scatter.31.cloned.1.call-update) | async-done | bytes 995344
  1942.7 2.7 copy.66
  1945.4 40.5 %reduce-scatter.35.cloned.1.call-done = f32[144,288]{1,0:T(8,128)} async-done(((f32[1152,288]{1,0:T(8,128)}), f32[144,288]{1,0:T(8,128)}) %reduce-scatter.35.cloned.1.call-update) | async-done | bytes 165904
  1985.9 60.8 %reduce-scatter.39.cloned.1.call-done = f32[144,1152]{1,0:T(8,128)} async-done(((f32[1152,1152]{1,0:T(8,128)}), f32[144,1152]{1,0:T(8,128)}) %reduce-scatter.39.cloned.1.call-update) | async-done | bytes 663568
  (202 shorter events, 20.5 us)
Async XLA Ops:
  7.2 278.5 %all-gather.7.cloned.1.call-start = ((), (), s32[]{:S(2)}) async-start(), calls=%async_computation.10 | async-start | bytes 19906560 | tf_op jit(solution)/shard_map/all_gather | solution.py:120
  7.9 420.3 %all-gather.9.cloned.1.call-start = ((), (), s32[]{:S(2)}) async-start(), calls=%async_computation.11 | async-start | bytes 9953280 | tf_op jit(solution)/shard_map/all_gather | solution.py:121
  8.7 474.8 %all-gather.11.cloned.1.call-start = ((), (), s32[]{:S(2)}) async-start(), calls=%async_computation.12 | async-start | bytes 3317760 | tf_op jit(solution)/shard_map/all_gather | solution.py:122
  9.4 1.3 copy-start.54
  9.4 3.9 copy-start.59
  9.4 4.1 copy-start.60
  9.4 4.4 copy-start.55
  9.4 4.6 copy-start.51
  9.5 27.4 %copy-start.52 = (bf16[1152]{0:T(1024)(128)(2,1)S(1)}, bf16[1152]{0:T(1024)(128)(2,1)}, u32[]{:S(2)}) copy-start(bf16[1152]{0:T(1024)(128)(2,1)} %param.25) | copy-start | bytes 6916
  9.5 45.0 %copy-start.56 = (s32[1,2]{1,0:T(1,128)S(1)}, s32[1,2]{1,0:T(1,128)}, u32[]{:S(2)}) copy-start(s32[1,2]{1,0:T(1,128)} %param.16) | copy-start | bytes 28
  9.5 47.5 %copy-start.2 = (bf16[1,256,1152]{2,1,0:T(8,128)(2,1)S(1)}, bf16[1,256,1152]{2,1,0:T(8,128)(2,1)}, u32[]{:S(2)}) copy-start(bf16[1,256,1152]{2,1,0:T(8,128)(2,1)} %param.14) | copy-start | bytes 1769476
  9.5 660.2 %all-gather.13.cloned.1.call-start = ((), (), s32[]{:S(2)}) async-start(), calls=%async_computation.13 | async-start | bytes 13271040 | tf_op jit(solution)/shard_map/all_gather | solution.py:123
  10.1 47.4 %copy-start.21 = (bf16[1,1152]{1,0:T(2,128)(2,1)S(1)}, bf16[1,1152]{1,0:T(2,128)(2,1)}, u32[]{:S(2)}) copy-start(bf16[1,1152]{1,0:T(2,128)(2,1)} %param.15) | copy-start | bytes 6916
  10.1 845.4 %all-gather.15.cloned.1.call-start = ((), (), s32[]{:S(2)}) async-start(), calls=%async_computation.14 | async-start | bytes 13271040 | tf_op jit(solution)/shard_map/all_gather | solution.py:124
  10.7 1023.3 %reduce-scatter.23.cloned.1.call-start = ((), (), s32[]{:S(2)}) async-start(), calls=%async_computation.16 | async-start | bytes 9953280 | tf_op jit(solution)/shard_map/reduce_scatter | solution.py:253
  56.4 381.9 %copy-start.47 = (pred[256]{0:T(512)(128)(4,1)}, pred[256]{0:T(512)(128)(4,1)S(1)}, u32[]{:S(2)}) copy-start(pred[256]{0:T(512)(128)(4,1)S(1)} %iota_compare_fusion) | copy-start | bytes 772
  57.1 371.1 %copy-start.38 = (f32[256]{0:T(256)}, f32[256]{0:T(256)S(1)}, u32[]{:S(2)}) copy-start(f32[256]{0:T(256)S(1)} %broadcast_multiply_fusion.1) | copy-start | bytes 3076
  57.4 236.0 %copy-start.42 = (f32[256]{0:T(256)}, f32[256]{0:T(256)S(1)}, u32[]{:S(2)}) copy-start(f32[256]{0:T(256)S(1)} %fusion.19) | copy-start | bytes 3076
  57.5 370.8 %copy-start.40 = (f32[256]{0:T(256)}, f32[256]{0:T(256)S(1)}, u32[]{:S(2)}) copy-start(f32[256]{0:T(256)S(1)} %fusion.45) | copy-start | bytes 3076
  58.1 235.3 %copy-start.23 = (f32[1,1152]{1,0:T(1,128)}, f32[1,1152]{1,0:T(1,128)S(1)}, u32[]{:S(2)}) copy-start(f32[1,1152]{1,0:T(1,128)S(1)} %get-tuple-element.81) | copy-start | bytes 13828
  294.2 140.1 %copy-start.27 = (f32[1152]{0:T(1024)}, f32[1152]{0:T(1024)S(1)}, u32[]{:S(2)}) copy-start(f32[1152]{0:T(1024)S(1)} %get-tuple-element.62) | copy-start | bytes 13828
  294.2 140.1 %copy-start.45 = (f32[1152]{0:T(1024)}, f32[1152]{0:T(1024)S(1)}, u32[]{:S(2)}) copy-start(f32[1152]{0:T(1024)S(1)} %get-tuple-element.61) | copy-start | bytes 13828
  435.6 3.7 copy-start.7
  438.3 2.0 copy-start
  855.4 10.1 copy-start.17
  855.4 10.1 copy-start.30
  855.4 10.1 copy-start.35
  865.5 8.8 copy-start.12
  865.5 8.9 copy-start.44
  874.3 2.5 copy-start.3
  874.3 1.5 copy-start.15
  874.3 1.5 copy-start.19
  874.3 1.5 copy-start.25
  874.4 1.5 copy-start.57
  874.4 3.3 copy-start.6
  874.8 2.1 copy-start.5
  874.8 2.0 copy-start.50
  881.7 4.3 copy-start.1
  881.7 4.3 copy-start.8
  881.7 4.3 copy-start.9
  881.7 4.3 copy-start.48
  886.0 4.9 copy-start.61
  889.6 2.1 copy-start.28
  889.6 2.1 copy-start.39
  889.6 2.1 copy-start.41
  889.7 2.1 copy-start.46
  897.6 319.6 %reduce-scatter.27.cloned.1.call-start = ((), (), s32[]{:S(2)}) async-start(), calls=%async_computation.18 | async-start | bytes 13271040 | tf_op jit(solution)/shard_map/reduce_scatter | solution.py:259
  906.9 2.7 copy-start.4
  907.0 581.1 %reduce-scatter.21.cloned.1.call-start = ((), (), s32[]{:S(2)}) async-start(), calls=%async_computation.15 | async-start | bytes 19906560 | tf_op jit(solution)/shard_map/reduce_scatter | solution.py:250
  919.6 1.9 copy-start.49
  944.9 598.8 %reduce-scatter.25.cloned.1.call-start = ((), (), s32[]{:S(2)}) async-start(), calls=%async_computation.17 | async-start | bytes 3317760 | tf_op jit(solution)/shard_map/reduce_scatter | solution.py:256
  948.4 777.5 %reduce-scatter.29.cloned.1.call-start = ((), (), s32[]{:S(2)}) async-start(), calls=%async_computation.19 | async-start | bytes 13271040 | tf_op jit(solution)/shard_map/reduce_scatter | solution.py:262
  960.1 827.6 %reduce-scatter.33.cloned.1.call-start = ((), (), s32[]{:S(2)}) async-start(), calls=%async_computation.21 | async-start | bytes 5971968
  1038.5 818.5 %reduce-scatter.37.cloned.1.call-start = ((), (), s32[]{:S(2)}) async-start(), calls=%async_computation.23 | async-start | bytes 7962624
  1222.7 720.0 %reduce-scatter.31.cloned.1.call-start = ((), (), s32[]{:S(2)}) async-start(), calls=%async_computation.20 | async-start | bytes 11943936
  1495.8 490.2 %reduce-scatter.35.cloned.1.call-start = ((), (), s32[]{:S(2)}) async-start(), calls=%async_computation.22 | async-start | bytes 1990656
  1546.4 500.3 %reduce-scatter.39.cloned.1.call-start = ((), (), s32[]{:S(2)}) async-start(), calls=%async_computation.24 | async-start | bytes 5971968
  1731.3 2.6 copy-start.53
  1731.3 2.7 copy-start.34
  1731.3 2.8 copy-start.32
  1731.3 2.9 copy-start.33
  1731.3 2.9 copy-start.37
  1731.3 45.8 %copy-start.22 = (bf16[1,1152]{1,0:T(2,128)(2,1)S(1)}, bf16[1,1152]{1,0:T(2,128)(2,1)}, u32[]{:S(2)}) copy-start(bf16[1,1152]{1,0:T(2,128)(2,1)} %param.15) | copy-start | bytes 6916
  1731.3 45.8 %copy-start.24 = (f32[1,1152]{1,0:T(1,128)S(1)}, f32[1,1152]{1,0:T(1,128)}, u32[]{:S(2)}) copy-start(f32[1,1152]{1,0:T(1,128)} %copy-done.23) | copy-start | bytes 13828
  (13 other events, 11.1 us)
Sparse Core Ops, SparseCore 0:
  9.6 276.1 all-gather.6
  287.3 140.9 all-gather.8
  429.8 53.5 all-gather.10
  484.9 184.8 all-gather.12
  671.1 184.2 all-gather.14
  897.7 136.2 reduce-scatter.22
  1036.5 180.6 reduce-scatter.26
  1219.6 268.4 reduce-scatter.20
  1490.5 53.2 reduce-scatter.24
  1546.1 179.7 reduce-scatter.28
  1729.3 58.3 reduce-scatter.32
  1791.5 65.4 reduce-scatter.36
  1860.5 82.1 reduce-scatter.30
  1946.5 39.4 reduce-scatter.34
  1989.8 56.9 reduce-scatter.38
where the time goes:
time: 2060 us; the launch traced here: 2050 us
  waiting for transfers between devices  1760 us (85%)
  matrix products  115 us (6%)
  blocking collectives  81.5 us (4%)
  local copies, waits for them, and re-layouts  52.8 us (3%)
  other arithmetic  22.1 us (1%)
    reduce_scatter x1, waiting for transfers between devices, body(): lax.psum_scatter(grad_w_ada.astype(jnp.bfloat16), 'fsdp', scatter_dimensi...  265 us
    unnamed x20, waiting for transfers between devices  255 us
    all_gather x1, waiting for transfers between devices, body(): lax.all_gather(w_ada, 'fsdp', axis=0, tiled=True)  228 us
    all_gather x1, waiting for transfers between devices, body(): lax.all_gather(w_up, 'fsdp', axis=0, tiled=True)  180 us
    reduce_scatter x1, waiting for transfers between devices, body(): lax.psum_scatter(grad_w_down.astype(jnp.bfloat16), 'fsdp', scatter_dimens...  179 us
    reduce_scatter x1, waiting for transfers between devices, body(): lax.psum_scatter(grad_w_up.astype(jnp.bfloat16), 'fsdp', scatter_dimensio...  179 us
    all_gather x1, waiting for transfers between devices, body(): lax.all_gather(w_down, 'fsdp', axis=0, tiled=True)  176 us
    all_gather x1, waiting for transfers between devices, body(): lax.all_gather(w_qkv, 'fsdp', axis=0, tiled=True)  134 us
  transfers between devices with their start and end apart: 15, of which 15 were waited for; matrix products, arithmetic and copies ran while one was open for 7% of the time, Pallas kernels for 0%

commit v1 on v0

--- a/solution.py
+++ b/solution.py
@@ -8,6 +8,27 @@
 epsilon = 1e-06
 masked_value = -1e30
 gelu_root = math.sqrt(2.0 / math.pi)
+
+
+def collect(array, axis, dim):
+    devices, index, extent = (lax.axis_size(axis), lax.axis_index(axis), array.shape[dim])
+    right = [(i, (i + 1) % devices) for i in range(devices)]
+    left = [(i, (i - 1) % devices) for i in range(devices)]
+    out = jnp.zeros((*array.shape[:dim], devices * extent, *array.shape[dim + 1 :]), array.dtype)
+    out = lax.dynamic_update_slice_in_dim(out, array, index * extent, axis=dim)
+    from_left = from_right = array
+    half = devices // 2
+    for hop in range(1, half + 1):
+        from_left = lax.ppermute(from_left, axis, right)
+        out = lax.dynamic_update_slice_in_dim(
+            out, from_left, (index - hop) % devices * extent, axis=dim
+        )
+        if hop < devices - half:
+            from_right = lax.ppermute(from_right, axis, left)
+            out = lax.dynamic_update_slice_in_dim(
+                out, from_right, (index + hop) % devices * extent, axis=dim
+            )
+    return out
 
 
 def layer_norm(values_in):
@@ -118,7 +139,7 @@
 ):
     weights_full = (
         lax.all_gather(w_ada, "fsdp", axis=0, tiled=True),
-        lax.all_gather(w_qkv, "fsdp", axis=0, tiled=True),
+        collect(w_qkv, "fsdp", 0),
         lax.all_gather(w_out, "fsdp", axis=0, tiled=True),
         lax.all_gather(w_up, "fsdp", axis=0, tiled=True),
         lax.all_gather(w_down, "fsdp", axis=0, tiled=True),

time: 2060 us -> 2170 us (1.053)
  blocking collectives: 81.5 us -> 372 us
  waiting for transfers between devices: 1760 us -> 1520 us
  matrix products: 115 us -> 137 us
    all_gather x1, waiting for transfers between devices: 228 us -> 26 us  [body(): lax.all_gather(w_ada, 'fsdp', axis=0, tiled=True)]
    all_gather x1, blocking collectives: 17 us -> 176 us  [body(): lax.all_gather(b_up, 'fsdp', axis=0, tiled=True)]
    unnamed x2, blocking collectives: 41 us -> 173 us
    unnamed x20, waiting for transfers between devices: 255 us -> 234 us
    dot_general x4 -> x7, matrix products: 30.9 us -> 52.2 us  [apply_rows(): jnp.einsum('isd,de->ise', left, right, preferred_element_type=jnp.float32)]
    unnamed x147 -> x195, local copies, waits for them, and re-layouts: 45.7 us -> 51.3 us
  transfers between devices with their start and end apart: 15 -> 18, of which waited for: 15 -> 14; matrix products, arithmetic and copies ran while one was open for 7% -> 9% of each run, Pallas kernels for 0% -> 0%
where the time goes in v1:
time: 2170 us
  waiting for transfers between devices  1520 us (70%)
  blocking collectives  372 us (17%)
  matrix products  137 us (6%)
  local copies, waits for them, and re-layouts  72.6 us (3%)
  other arithmetic  27.3 us (1%)
    reduce_scatter x1, waiting for transfers between devices, body(): lax.psum_scatter(grad_w_ada.astype(jnp.bfloat16), 'fsdp', scatter_dimensi...  265 us
    unnamed x20, waiting for transfers between devices  234 us
    all_gather x1, waiting for transfers between devices, body(): lax.all_gather(w_up, 'fsdp', axis=0, tiled=True)  182 us
    reduce_scatter x1, waiting for transfers between devices, body(): lax.psum_scatter(grad_w_down.astype(jnp.bfloat16), 'fsdp', scatter_dimens...  179 us
    reduce_scatter x1, waiting for transfers between devices, body(): lax.psum_scatter(grad_w_up.astype(jnp.bfloat16), 'fsdp', scatter_dimensio...  179 us
    all_gather x1, waiting for transfers between devices, body(): lax.all_gather(w_down, 'fsdp', axis=0, tiled=True)  177 us
    all_gather x1, blocking collectives, body(): lax.all_gather(b_up, 'fsdp', axis=0, tiled=True)  176 us
    unnamed x2, blocking collectives  173 us
  transfers between devices with their start and end apart: 18, of which 14 were waited for; matrix products, arithmetic and copies ran while one was open for 9% of the time, Pallas kernels for 0%

profile of v1, /device:TPU:0, one launch (start us, length us, event | category | flops | bytes accessed | tf_op | source)
XLA Modules:
  0.0 2167.0 jit_solution(12176518160756075870)
XLA Ops:
  11.0 3.0 collective-permute-start
  14.0 2.0 collective-permute-start.1
  17.9 175.6 %all-gather = bf16[4,1,1152]{2,1,0:T(2,128)(2,1)S(1)} all-gather(bf16[1,1,1152]{2,1,0:T(2,128)(2,1)S(1)} %reshape.580), channel_id=1, replica_groups=mesh['dp'=8,'fsdp'=4] {'fsdp'}, dimensions={0}, use_global_device_ids=true | all-gather | bytes 11520 | tf_op jit(solution)/shard_map/all_gather | solution.py:149
  194.7 7.8 collective-permute-start.2
  206.7 153.7 %all-reduce.11 = (bf16[2304]{0:T(1024)(128)(2,1)S(1)}, bf16[6912]{0:T(1024)(128)(2,1)S(1)}, bf16[1152]{0:T(1024)(128)(2,1)S(1)}, bf16[1152]{0:T(1024)(128)(2,1)}) all-reduce(bf16[2304]{0:T(1024)(128)(2,1)S(1)} %dynamic-update-slice.1, bf16[6912]{0:T(1024)(128)(2,1)S(1)} %dynamic-update-slice, ...), channel_id=1, replica_groups=mesh['dp'=8,'fsdp'=4] {'fsdp'}, use_global_device_ids=true, to_apply=%add.1 | all-reduce | flops 11520 | bytes 46080
  362.2 3.7 broadcast_in_dim.26
  365.9 1.5 constant_dynamic-update-slice_fusion.3
  367.4 3.0 constant_dynamic-update-slice_fusion.2
  370.4 3.0 constant_dynamic-update-slice_fusion.1
  373.4 3.1 constant_dynamic-update-slice_fusion
  376.4 26.0 %all-gather.7.cloned.1.call-done = bf16[1152,6912]{1,0:T(8,128)(2,1)} async-done(((bf16[288,6912]{1,0:T(8,128)(2,1)}), bf16[1152,6912]{1,0:T(8,128)(2,1)}) %all-gather.7.cloned.1.call-update) | async-done | bytes 15925264 | tf_op jit(solution)/shard_map/all_gather | solution.py:141
  402.5 7.7 convolution_reduce_fusion
  410.9 6.8 convolution_bitcast_fusion.1
  417.7 1.8 copy-done.13
  419.6 126.3 %all-gather.15.cloned.1.call-done = bf16[1152,3456]{1,0:T(8,128)(2,1)} async-done(((bf16[288,3456]{1,0:T(8,128)(2,1)}), bf16[1152,3456]{1,0:T(8,128)(2,1)}) %all-gather.15.cloned.1.call-update) | async-done | bytes 7962640 | tf_op jit(solution)/shard_map/all_gather | solution.py:169
  546.0 6.1 convolution_bitcast_fusion
  556.4 2.4 fusion.11
  561.5 2.1 copy-done
  564.7 36.5 %all-gather.9.cloned.1.call-done = bf16[1152,1152]{1,0:T(8,128)(2,1)} async-done(((bf16[288,1152]{1,0:T(8,128)(2,1)}), bf16[1152,1152]{1,0:T(8,128)(2,1)}) %all-gather.9.cloned.1.call-update) | async-done | bytes 2654224 | tf_op jit(solution)/shard_map/all_gather | solution.py:143
  601.2 3.9 fusion.99
  605.4 182.1 %all-gather.11.cloned.1.call-done = bf16[1152,4608]{1,0:T(8,128)(2,1)} async-done(((bf16[288,4608]{1,0:T(8,128)(2,1)}), bf16[1152,4608]{1,0:T(8,128)(2,1)}) %all-gather.11.cloned.1.call-update) | async-done | bytes 10616848 | tf_op jit(solution)/shard_map/all_gather | solution.py:144
  787.5 9.1 convolution_add_fusion
  796.6 176.5 %all-gather.13.cloned.1.call-done = bf16[4608,1152]{1,0:T(8,128)(2,1)} async-done(((bf16[1152,1152]{1,0:T(8,128)(2,1)}), bf16[4608,1152]{1,0:T(8,128)(2,1)}) %all-gather.13.cloned.1.call-update) | async-done | bytes 10616848 | tf_op jit(solution)/shard_map/all_gather | solution.py:145
  973.2 10.5 fusion.104
  983.7 3.9 fusion.47
  991.0 1.9 convolution_convert_fusion.4
  992.8 2.1 copy.67
  994.9 4.3 bitcast_reduce_fusion
  999.3 1.5 multiply_reduce_fusion
  1005.0 5.9 convolution_convert_fusion.2
  1011.6 8.7 convolution_convert_fusion.1
  1023.8 7.0 fusion.42
  1031.4 1.5 dynamic-update-slice.4
  1034.2 1.9 fusion.40
  1036.1 1.5 dynamic-update-slice.5
  1038.2 3.4 fusion.48
  1041.6 1.5 dynamic-update-slice.6
  1043.1 1.4 dynamic-update-slice.7
  1045.9 9.0 fusion.37
  1055.2 5.9 multiply_convert_fusion
  1062.3 2.4 convolution_convert_fusion.3
  1065.5 10.8 convolution_convert_fusion
  1076.3 71.0 %reduce-scatter.23.cloned.1.call-done = bf16[288,3456]{1,0:T(8,128)(2,1)} async-done(((bf16[1152,3456]{1,0:T(8,128)(2,1)}), bf16[288,3456]{1,0:T(8,128)(2,1)}) %reduce-scatter.23.cloned.1.call-update) | async-done | bytes 1990672 | tf_op jit(solution)/shard_map/reduce_scatter | solution.py:274
  1147.4 4.5 copy.80
  1152.0 178.6 %reduce-scatter.27.cloned.1.call-done = bf16[288,4608]{1,0:T(8,128)(2,1)} async-done(((bf16[1152,4608]{1,0:T(8,128)(2,1)}), bf16[288,4608]{1,0:T(8,128)(2,1)}) %reduce-scatter.27.cloned.1.call-update) | async-done | bytes 2654224 | tf_op jit(solution)/shard_map/reduce_scatter | solution.py:280
  1330.6 5.5 copy.84
  1336.1 265.3 %reduce-scatter.21.cloned.1.call-done = bf16[288,6912]{1,0:T(8,128)(2,1)} async-done(((bf16[1152,6912]{1,0:T(8,128)(2,1)}), bf16[288,6912]{1,0:T(8,128)(2,1)}) %reduce-scatter.21.cloned.1.call-update) | async-done | bytes 3981328 | tf_op jit(solution)/shard_map/reduce_scatter | solution.py:271
  1601.5 7.7 copy.78
  1609.2 47.9 %reduce-scatter.25.cloned.1.call-done = bf16[288,1152]{1,0:T(8,128)(2,1)} async-done(((bf16[1152,1152]{1,0:T(8,128)(2,1)}), bf16[288,1152]{1,0:T(8,128)(2,1)}) %reduce-scatter.25.cloned.1.call-update) | async-done | bytes 663568 | tf_op jit(solution)/shard_map/reduce_scatter | solution.py:277
  1657.1 2.7 copy.82
  1659.8 179.4 %reduce-scatter.29.cloned.1.call-done = bf16[1152,1152]{1,0:T(8,128)(2,1)} async-done(((bf16[4608,1152]{1,0:T(8,128)(2,1)}), bf16[1152,1152]{1,0:T(8,128)(2,1)}) %reduce-scatter.29.cloned.1.call-update) | async-done | bytes 2654224 | tf_op jit(solution)/shard_map/reduce_scatter | solution.py:283
  1839.3 5.4 copy.86
  1847.8 19.2 all-reduce.10
  1867.3 23.7 %all-reduce.9 = (f32[1728]{0:T(1024)}, f32[576]{0:T(1024)}, f32[288]{0:T(512)}, f32[1152]{0:T(1024)}, f32[288]{0:T(512)}) all-reduce(f32[1728]{0:T(1024)S(1)} %dynamic-slice_convert_fusion.1, f32[576]{0:T(1024)S(1)} %dynamic-slice_convert_fusion.2, f32[288]{0:T(512)S(1)} %get-tuple-element.116, ...), channel_id=1, replica_groups=mesh['dp'=8,'fsdp'=4] {'dp'}, use_global_device_ids=true, to_apply=%region_30.31 | all-reduce | flops 4032 | bytes 32256 | tf_op jit(solution)/shard_map/psum | solution.py:309
  1891.1 3.4 fusion.36
  1896.1 10.5 fusion.72
  1906.6 16.1 fusion.21
  1922.7 2.1 copy.81
  1924.9 45.5 %reduce-scatter.37.cloned.1.call-done = f32[576,288]{1,0:T(8,128)} async-done(((f32[4608,288]{1,0:T(8,128)}), f32[576,288]{1,0:T(8,128)}) %reduce-scatter.37.cloned.1.call-update) | async-done | bytes 663568
  1970.4 2.3 copy.85
  1972.7 83.4 %reduce-scatter.31.cloned.1.call-done = f32[864,288]{1,0:T(8,128)} async-done(((f32[6912,288]{1,0:T(8,128)}), f32[864,288]{1,0:T(8,128)}) %reduce-scatter.31.cloned.1.call-update) | async-done | bytes 995344
  2056.1 2.7 copy.79
  2058.8 40.5 %reduce-scatter.35.cloned.1.call-done = f32[144,288]{1,0:T(8,128)} async-done(((f32[1152,288]{1,0:T(8,128)}), f32[144,288]{1,0:T(8,128)}) %reduce-scatter.35.cloned.1.call-update) | async-done | bytes 165904
  2099.4 60.8 %reduce-scatter.39.cloned.1.call-done = f32[144,1152]{1,0:T(8,128)} async-done(((f32[1152,1152]{1,0:T(8,128)}), f32[144,1152]{1,0:T(8,128)}) %reduce-scatter.39.cloned.1.call-update) | async-done | bytes 663568
  (274 shorter events, 39.1 us)
Async XLA Ops:
  7.2 395.3 %all-gather.7.cloned.1.call-start = ((), (), s32[]{:S(2)}) async-start(), calls=%async_computation.10 | async-start | bytes 19906560 | tf_op jit(solution)/shard_map/all_gather | solution.py:141
  7.9 538.1 %all-gather.15.cloned.1.call-start = ((), (), s32[]{:S(2)}) async-start(), calls=%async_computation.14 | async-start | bytes 9953280 | tf_op jit(solution)/shard_map/all_gather | solution.py:169
  8.7 592.5 %all-gather.9.cloned.1.call-start = ((), (), s32[]{:S(2)}) async-start(), calls=%async_computation.11 | async-start | bytes 3317760 | tf_op jit(solution)/shard_map/all_gather | solution.py:143
  9.4 6.6 copy-start.76
  9.4 6.6 copy-start.81
  9.4 184.2 %copy-start.3 = (bf16[1,256,1152]{2,1,0:T(8,128)(2,1)S(1)}, bf16[1,256,1152]{2,1,0:T(8,128)(2,1)}, u32[]{:S(2)}) copy-start(bf16[1,256,1152]{2,1,0:T(8,128)(2,1)} %param.14) | copy-start | bytes 1769476
  9.4 778.0 %all-gather.11.cloned.1.call-start = ((), (), s32[]{:S(2)}) async-start(), calls=%async_computation.12 | async-start | bytes 13271040 | tf_op jit(solution)/shard_map/all_gather | solution.py:144
  10.0 193.0 %copy-start.79 = (u32[32]{0:T(128)S(1)}, u32[32]{0:T(128)}, u32[]{:S(2)}) copy-start(u32[32]{0:T(128)} %constant.85) | copy-start | bytes 388
  10.0 195.6 %copy-start.82 = (bf16[288]{0:T(512)(128)(2,1)S(1)}, bf16[288]{0:T(512)(128)(2,1)}, u32[]{:S(2)}) copy-start(bf16[288]{0:T(512)(128)(2,1)} %param.24) | copy-start | bytes 1732
  10.0 195.8 %copy-start.83 = (bf16[288]{0:T(512)(128)(2,1)S(1)}, bf16[288]{0:T(512)(128)(2,1)}, u32[]{:S(2)}) copy-start(bf16[288]{0:T(512)(128)(2,1)} %param.26) | copy-start | bytes 1732
  10.0 196.1 %copy-start.80 = (bf16[576]{0:T(1024)(128)(2,1)S(1)}, bf16[576]{0:T(1024)(128)(2,1)}, u32[]{:S(2)}) copy-start(bf16[576]{0:T(1024)(128)(2,1)} %param.23) | copy-start | bytes 3460
  10.1 196.3 %copy-start.77 = (bf16[1728]{0:T(1024)(128)(2,1)S(1)}, bf16[1728]{0:T(1024)(128)(2,1)}, u32[]{:S(2)}) copy-start(bf16[1728]{0:T(1024)(128)(2,1)} %param.22) | copy-start | bytes 10372
  10.1 351.5 %copy-start.40 = (bf16[1,1152]{1,0:T(2,128)(2,1)S(1)}, bf16[1,1152]{1,0:T(2,128)(2,1)}, u32[]{:S(2)}) copy-start(bf16[1,1152]{1,0:T(2,128)(2,1)} %param.15) | copy-start | bytes 6916
  10.1 963.1 %all-gather.13.cloned.1.call-start = ((), (), s32[]{:S(2)}) async-start(), calls=%async_computation.13 | async-start | bytes 13271040 | tf_op jit(solution)/shard_map/all_gather | solution.py:145
  10.7 1136.7 %reduce-scatter.23.cloned.1.call-start = ((), (), s32[]{:S(2)}) async-start(), calls=%async_computation.16 | async-start | bytes 9953280 | tf_op jit(solution)/shard_map/reduce_scatter | solution.py:274
  11.0 183.7 %collective-permute-start = (bf16[288,3456]{1,0:T(8,128)(2,1)S(1)}, bf16[288,3456]{1,0:T(8,128)(2,1)}, u32[]{:S(2)}, u32[]{:S(2)}) collective-permute-start(bf16[288,3456]{1,0:T(8,128)(2,1)S(1)} %copy-done.4), channel_id=1, source_target_pairs={{0,1},{1,2},{2,3},{3,0},{4,5},{5,6},{6,7},{7,4},{8,9},{9,10},{10,1... | collective-permute-start | bytes 5971976 | tf_op jit(solution)/shard_map/ppermute | solution.py:22
  14.0 356.4 %collective-permute-start.1 = (bf16[288,3456]{1,0:T(8,128)(2,1)S(1)}, bf16[288,3456]{1,0:T(8,128)(2,1)}, u32[]{:S(2)}, u32[]{:S(2)}) collective-permute-start(bf16[288,3456]{1,0:T(8,128)(2,1)S(1)} %copy-done.4), channel_id=1, source_target_pairs={{0,3},{1,0},{2,1},{3,2},{4,7},{5,4},{6,5},{7,6},{8,11},{9,8},{10,9... | collective-permute-start | bytes 5971976 | tf_op jit(solution)/shard_map/ppermute | solution.py:27
  193.8 352.2 %copy-start.53 = (f32[256]{0:T(256)}, f32[256]{0:T(256)S(1)}, u32[]{:S(2)}) copy-start(f32[256]{0:T(256)S(1)} %broadcast_multiply_fusion.2) | copy-start | bytes 3076
  194.6 11.7 copy-start.65
  194.7 351.3 %copy-start.55 = (f32[256]{0:T(256)}, f32[256]{0:T(256)S(1)}, u32[]{:S(2)}) copy-start(f32[256]{0:T(256)S(1)} %fusion.77) | copy-start | bytes 3076
  194.7 178.7 %collective-permute-start.2 = (bf16[288,3456]{1,0:T(8,128)(2,1)}, bf16[288,3456]{1,0:T(8,128)(2,1)}, u32[]{:S(2)}, u32[]{:S(2)}) collective-permute-start(bf16[288,3456]{1,0:T(8,128)(2,1)} %collective-permute-done), channel_id=1, source_target_pairs={{0,1},{1,2},{2,3},{3,0},{4,5},{5,6},{6,7},{7,4},{8,9},{9,10},{10,1... | collective-permute-start | bytes 5971976 | tf_op jit(solution)/shard_map/ppermute | solution.py:22
  362.2 40.3 %copy-start.42 = (f32[1,1152]{1,0:T(1,128)}, f32[1,1152]{1,0:T(1,128)S(1)}, u32[]{:S(2)}) copy-start(f32[1,1152]{1,0:T(1,128)S(1)} %get-tuple-element.79) | copy-start | bytes 13828
  410.9 135.1 %copy-start.35 = (f32[1152]{0:T(1024)}, f32[1152]{0:T(1024)S(1)}, u32[]{:S(2)}) copy-start(f32[1152]{0:T(1024)S(1)} %get-tuple-element.60) | copy-start | bytes 13828
  410.9 135.1 %copy-start.66 = (f32[1152]{0:T(1024)}, f32[1152]{0:T(1024)S(1)}, u32[]{:S(2)}) copy-start(f32[1152]{0:T(1024)S(1)} %get-tuple-element.59) | copy-start | bytes 13828
  546.0 6.2 copy-start.14
  555.8 5.6 copy-start.16
  556.1 4.6 copy-start.5
  564.7 40.4 %copy-start.9 = (bf16[16,72,256]{2,1,0:T(8,128)(2,1)}, bf16[16,72,256]{2,1,0:T(8,128)(2,1)S(1)}, u32[]{:S(2)}) copy-start(bf16[16,72,256]{2,1,0:T(8,128)(2,1)S(1)} %convolution_convert_fusion.6) | copy-start | bytes 1769476
  601.2 186.3 %copy-start.28 = (f32[1152]{0:T(1024)S(1)}, f32[1152]{0:T(1024)}, u32[]{:S(2)}) copy-start(f32[1152]{0:T(1024)} %get-tuple-element.58) | copy-start | bytes 13828
  601.2 186.3 %copy-start.37 = (f32[1152]{0:T(1024)S(1)}, f32[1152]{0:T(1024)}, u32[]{:S(2)}) copy-start(f32[1152]{0:T(1024)} %get-tuple-element.57) | copy-start | bytes 13828
  601.2 186.3 %copy-start.51 = (f32[4608]{0:T(1024)S(1)}, f32[4608]{0:T(1024)}, u32[]{:S(2)}) copy-start(f32[4608]{0:T(1024)} %reshape.582) | copy-start | bytes 55300
  605.1 378.6 %copy-start.49 = (f32[256]{0:T(256)}, f32[256]{0:T(256)S(1)}, u32[]{:S(2)}) copy-start(f32[256]{0:T(256)S(1)} %broadcast_multiply_fusion) | copy-start | bytes 3076
  605.4 378.3 %copy-start.60 = (f32[256]{0:T(256)}, f32[256]{0:T(256)S(1)}, u32[]{:S(2)}) copy-start(f32[256]{0:T(256)S(1)} %fusion.78) | copy-start | bytes 3076
  787.5 185.7 %copy-start.19 = (bf16[1,256,1152]{2,1,0:T(8,128)(2,1)S(1)}, bf16[1,256,1152]{2,1,0:T(8,128)(2,1)}, u32[]{:S(2)}) copy-start(bf16[1,256,1152]{2,1,0:T(8,128)(2,1)} %param.27) | copy-start | bytes 1769476
  787.5 185.7 %copy-start.44 = (f32[1152]{0:T(1024)S(1)}, f32[1152]{0:T(1024)}, u32[]{:S(2)}) copy-start(f32[1152]{0:T(1024)} %get-tuple-element.56) | copy-start | bytes 13828
  787.5 185.7 %copy-start.73 = (f32[256]{0:T(256)S(1)}, f32[256]{0:T(256)}, u32[]{:S(2)}) copy-start(f32[256]{0:T(256)} %fusion.87) | copy-start | bytes 3076
  973.2 10.5 copy-start.84
  983.7 3.9 copy-start.24
  983.7 3.9 copy-start.29
  994.9 4.3 copy-start.1
  994.9 4.3 copy-start.17
  994.9 4.3 copy-start.18
  994.9 4.3 copy-start.71
  999.3 4.9 copy-start.85
  1010.9 319.6 %reduce-scatter.27.cloned.1.call-start = ((), (), s32[]{:S(2)}) async-start(), calls=%async_computation.18 | async-start | bytes 13271040 | tf_op jit(solution)/shard_map/reduce_scatter | solution.py:280
  1020.4 581.1 %reduce-scatter.21.cloned.1.call-start = ((), (), s32[]{:S(2)}) async-start(), calls=%async_computation.15 | async-start | bytes 19906560 | tf_op jit(solution)/shard_map/reduce_scatter | solution.py:271
  1030.8 7.4 copy-start.21
  1045.9 9.0 copy-start.32
  1045.9 9.2 copy-start.48
  1061.1 596.0 %reduce-scatter.25.cloned.1.call-start = ((), (), s32[]{:S(2)}) async-start(), calls=%async_computation.17 | async-start | bytes 3317760 | tf_op jit(solution)/shard_map/reduce_scatter | solution.py:277
  1064.8 774.5 %reduce-scatter.29.cloned.1.call-start = ((), (), s32[]{:S(2)}) async-start(), calls=%async_computation.19 | async-start | bytes 13271040 | tf_op jit(solution)/shard_map/reduce_scatter | solution.py:283
  1076.3 846.5 %reduce-scatter.33.cloned.1.call-start = ((), (), s32[]{:S(2)}) async-start(), calls=%async_computation.21 | async-start | bytes 5971968
  1151.9 818.5 %reduce-scatter.37.cloned.1.call-start = ((), (), s32[]{:S(2)}) async-start(), calls=%async_computation.23 | async-start | bytes 7962624
  1336.1 720.0 %reduce-scatter.31.cloned.1.call-start = ((), (), s32[]{:S(2)}) async-start(), calls=%async_computation.20 | async-start | bytes 11943936
  1609.1 490.2 %reduce-scatter.35.cloned.1.call-start = ((), (), s32[]{:S(2)}) async-start(), calls=%async_computation.22 | async-start | bytes 1990656
  1659.8 500.4 %reduce-scatter.39.cloned.1.call-start = ((), (), s32[]{:S(2)}) async-start(), calls=%async_computation.24 | async-start | bytes 5971968
  1844.7 46.4 %copy-start.72 = (pred[256]{0:T(512)(128)(4,1)S(1)}, pred[256]{0:T(512)(128)(4,1)}, u32[]{:S(2)}) copy-start(pred[256]{0:T(512)(128)(4,1)} %iota_compare_fusion) | copy-start | bytes 772
  1891.0 3.5 copy-start.12
  1891.1 3.5 copy-start.34
  1891.1 3.5 copy-start.47
  1896.0 10.6 copy-start.31
  1896.1 10.6 copy-start.39
  1896.1 10.6 copy-start.52
  1896.1 10.6 copy-start.68
  (40 other events, 72.0 us)
Sparse Core Ops, SparseCore 0:
  9.6 392.8 all-gather.6
  404.1 141.8 all-gather.14
  547.6 53.5 all-gather.8
  602.6 184.8 all-gather.10
  788.9 184.2 all-gather.12
  1011.1 136.2 reduce-scatter.22
  1149.8 180.6 reduce-scatter.26
  1333.0 268.4 reduce-scatter.20
  1603.9 53.2 reduce-scatter.24
  1659.4 179.8 reduce-scatter.28
  1842.7 58.3 reduce-scatter.32
  1904.9 65.4 reduce-scatter.36
  1973.9 82.1 reduce-scatter.30
  2059.9 39.4 reduce-scatter.34
  2103.2 56.9 reduce-scatter.38
